TPU v7x, 512 devices: a whole 4x4x16 slice. The times are simulated.
512 devices in a mesh: gz: 16 (over z), xy: 32 (over x, y, core).
Axes of the slice: x: 4, y: 4, z: 16, core: 2. Of those that a mesh axis runs over, the one named last changes fastest.
Arguments:
- source: float32 [512, 128, 512], P('gz', 'xy'), may hold values from -6 to 6
- potential: float32 [512, 128, 512], P('gz', 'xy'), may hold values from -6 to 6
Outputs:
- new_potential: float32 [512, 128, 512], P('gz', 'xy')
All inputs are finite; a program needn't handle non-finite values.
Results may differ from a plain program's by a relative error of at most 0.0003.
Values sent between devices are 32-bit elements; how exact they have to be, the bound alone decides.
A program may use at most 64 MiB of HBM per device.

v0:
```python
import math
import jax
import jax.numpy as jnp
from jax import lax
from jax.sharding import PartitionSpec as P

SWEEPS = 2
SCREEN = 64
OMEGA = 0.8
HIGH = lax.Precision.HIGHEST


def with_halo(value, sides, width):
    for axis, dim in sides:
        size, length = (lax.axis_size(axis), value.shape[dim])
        up = [(i, (i + 1) % size) for i in range(size - 1)]
        down = [(j, i) for i, j in up]
        last = lax.slice_in_dim(value, length - width, length, axis=dim)
        initial = lax.slice_in_dim(value, 0, width, axis=dim)
        before = lax.ppermute(last, axis, up)
        after = lax.ppermute(initial, axis, down)
        value = jnp.concatenate([before, value, after], axis=dim)
    return value


def carried_in(value, axis, join, neutral, backward):
    count, mine = (lax.axis_size(axis), lax.axis_index(axis))
    pieces = jax.tree.map(lambda part: lax.all_gather(part, axis), value)
    if backward:
        pieces = jax.tree.map(lambda part: part[::-1], pieces)
        mine = count - 1 - mine
    total = jax.tree.map(
        lambda part, zero: jnp.full_like(part, 0) + jnp.asarray(zero, part.dtype), value, neutral
    )

    def step(position, total):
        longer = join(total, jax.tree.map(lambda part: part[position], pieces))
        return jax.tree.map(lambda new, old: jnp.where(position < mine, new, old), longer, total)

    return lax.fori_loop(0, count - 1, step, total)


def sine_table(count):
    idx = jnp.arange(1, count + 1, dtype=jnp.int32)
    turns = idx[:, None] * idx[None, :] % (2 * (count + 1))
    return math.sqrt(2.0 / (count + 1)) * jnp.sin(math.pi / (count + 1) * turns.astype(jnp.float32))


def eigenvalues(count, taken):
    idx = (jnp.arange(taken, dtype=jnp.int32) + 1).astype(jnp.float32)
    return 2.0 - 2.0 * jnp.cos(math.pi / (count + 1) * idx)


def relax(extended, rhs, kappa):
    centre = extended[1:-1, 1:-1]
    padded_y = jnp.pad(centre, ((0, 0), (0, 0), (1, 1)))
    total = extended[2:, 1:-1] + extended[:-2, 1:-1] + extended[1:-1, 2:] + extended[1:-1, :-2]
    total = total + padded_y[:, :, 2:] + padded_y[:, :, :-2]
    centre_weight = 6.0 + kappa
    return centre + OMEGA * (rhs - (centre_weight * centre - total)) / centre_weight


def smooth(field, source, kappa):
    for sweep in range(SWEEPS):
        extended = with_halo(field, (("gz", 0), ("xy", 1)), 1)
        field = relax(extended, source, kappa)
    return field


def compose(earlier, later):
    return (earlier[0] * later[0], later[0] * earlier[1] + later[1])


def solve_columns(rhs, diag):
    planes = rhs.shape[0]
    first = lax.axis_index("gz") * planes
    decay = jnp.log(0.5 * diag + jnp.sqrt(0.25 * diag * diag - 1.0))
    factor = jnp.exp(-decay)
    level = (first + jnp.arange(planes, dtype=jnp.int32)).astype(jnp.float32)
    level = level.reshape((planes,) + (1,) * diag.ndim)
    coeff = (
        factor * jnp.expm1(-2.0 * (level + 1.0) * decay) / jnp.expm1(-2.0 * (level + 2.0) * decay)
    )
    ones = jnp.ones_like(diag)
    zeros = jnp.zeros_like(diag)

    def up_step(carry, item):
        pivot, value = item
        return ((pivot * carry[0], pivot * (value + carry[1])), None)

    (lift, offset), unused = lax.scan(up_step, (ones, zeros), (coeff, rhs))
    prefix = carried_in((lift, offset), "gz", compose, (ones, zeros), False)

    def fill_up(carry, item):
        pivot, value = item
        carry = pivot * (value + carry)
        return (carry, carry)

    unused, eliminated = lax.scan(fill_up, prefix[1], (coeff, rhs))

    def down_step(carry, item):
        pivot, value = item
        return ((pivot * carry[0], value + pivot * carry[1]), None)

    (lift_top, offset_top), unused = lax.scan(
        down_step, (ones, zeros), (coeff, eliminated), reverse=True
    )
    suffix = carried_in((lift_top, offset_top), "gz", compose, (ones, zeros), True)

    def fill_down(carry, item):
        pivot, value = item
        carry = value + pivot * carry
        return (carry, carry)

    unused, solved = lax.scan(fill_down, suffix[1], (coeff, eliminated), reverse=True)
    return solved


def coarse_solve(coarse, kappa):
    planes, rows, cols = coarse.shape
    groups = lax.axis_size("xy")
    total_rows = rows * groups
    table_x = sine_table(total_rows)
    table_y = sine_table(cols)
    modes_x = eigenvalues(total_rows, total_rows)
    whole = lax.all_gather(coarse, "xy", axis=1, tiled=True)
    spec = jnp.dot(whole.reshape(-1, cols), table_y, precision=HIGH).reshape(
        planes, total_rows, cols
    )
    spec = jnp.einsum("ax,zxy->zay", table_x, spec, precision=HIGH)
    modes_y = eigenvalues(cols, cols)
    diag = 2.0 + modes_x[:, None] + modes_y[None, :] + 4.0 * kappa
    solved = solve_columns(4.0 * spec, diag)
    own_rows = lax.dynamic_slice_in_dim(table_x, lax.axis_index("xy") * rows, rows, 0)
    back = jnp.einsum("xa,zay->zxy", own_rows, solved, precision=HIGH)
    return jnp.dot(back.reshape(-1, cols), table_y, precision=HIGH).reshape(planes, rows, cols)


def body(source, potential):
    kappa = 1.0 / (SCREEN * SCREEN)
    centre_weight = 6.0 + kappa
    height, width, depth_y = source.shape
    field = smooth(potential, source, kappa)
    extended = with_halo(field, (("gz", 0), ("xy", 1)), 1)
    padded_y = jnp.pad(field, ((0, 0), (0, 0), (1, 1)))
    total = extended[2:, 1:-1] + extended[:-2, 1:-1] + extended[1:-1, 2:] + extended[1:-1, :-2]
    total = total + padded_y[:, :, 2:] + padded_y[:, :, :-2]
    residual = source - (centre_weight * field - total)
    coarse = residual.reshape(height // 2, 2, width // 2, 2, depth_y // 2, 2).mean(axis=(1, 3, 5))
    correction = coarse_solve(coarse, kappa)
    lifted = jnp.broadcast_to(
        correction[:, None, :, None, :, None], (height // 2, 2, width // 2, 2, depth_y // 2, 2)
    )
    field = field + lifted.reshape(height, width, depth_y)
    return smooth(field, source, kappa)


def solution(mesh):
    placed = (P("gz", "xy", None), P("gz", "xy", None))
    return jax.shard_map(
        body, mesh=mesh, in_specs=placed, out_specs=P("gz", "xy", None), check_vma=False
    )
```

profile of v0, /device:TPU:134, one launch (start us, length us, event | category | flops | bytes accessed | tf_op | source)
XLA Modules:
  0.0 558.7 jit_solution(7522685730354100004)
XLA Ops:
  9.3 3.8 collective-permute-start.1
  16.1 3.4 collective-permute-start.2
  21.5 5.8 %collective-permute-done.3 = f32[34,1,512]{2,0,1:T(8,128)S(1)} collective-permute-done((f32[34,1,512]{2,0,1:T(8,128)S(1)}, f32[34,1,512]{2,0,1:T(8,128)S(1)}, u32[]{:S(2)}, u32[]{:S(2)}) %collective-permute-start.3) | collective-permute-done | bytes 69664 | tf_op jit(solution)/shard_map/ppermute | solution.py:20
  30.8 3.6 collective-permute-start.5
  34.5 3.1 collective-permute-done.5
  39.6 2.4 collective-permute-start.7
  42.0 5.4 collective-permute-done.7
  50.6 3.9 collective-permute-start.9
  54.5 2.8 collective-permute-done.9
  59.3 2.4 collective-permute-start.11
  61.7 5.4 collective-permute-done.11
  68.4 18.1 %reshape.130 = f32[16,2,2,2,256,2]{5,4,1,0,3,2:T(8,128)} reshape(f32[32,4,512]{2,0,1:T(8,128)S(1)} %fusion.23) | data formatting | bytes 524288 | tf_op jit(solution)/shard_map/reshape | solution.py:149
  86.5 7.0 %reduce_sum.9 = f32[16,2,256]{2,0,1:T(8,128)S(1)} reduce(f32[16,2,2,2,256,2]{5,4,1,0,3,2:T(8,128)} %reshape.130, f32[]{:T(128)} %constant.201.clone.1), dimensions={1,3,5}, to_apply=%region_0.1 | reduce | flops 57344 | bytes 294916 | tf_op jit(solution)/shard_map/reduce_sum | solution.py:149
  95.2 56.8 %all-gather.10.cloned.1.call-done = f32[16,64,256]{2,0,1:T(8,128)} async-done(((f32[16,2,256]{2,0,1:T(8,128)}), f32[16,64,256]{2,0,1:T(8,128)}) %all-gather.10.cloned.1.call-update) | async-done | bytes 1048592 | tf_op jit(solution)/shard_map/all_gather | solution.py:126
  152.0 3.8 fusion.6
  159.5 67.3 %all-gather.14.cloned.1.call-done = f32[1024,256]{1,0:T(8,128)} async-done(((f32[64,256]{1,0:T(8,128)}), f32[1024,256]{1,0:T(8,128)}) %all-gather.14.cloned.1.call-update) | async-done | bytes 1048592 | tf_op jit(solution)/shard_map/all_gather | solution.py:28
  226.8 70.0 %all-gather.12.cloned.1.call-done = f32[1024,256]{1,0:T(8,128)} async-done(((f32[64,256]{1,0:T(8,128)}), f32[1024,256]{1,0:T(8,128)}) %all-gather.12.cloned.1.call-update) | async-done | bytes 1048592 | tf_op jit(solution)/shard_map/all_gather | solution.py:28
  296.8 14.0 %while.89 = (s32[]{:T(128)}, f32[64,256]{1,0:T(8,128)S(1)}, s32[]{:T(128)}, f32[16,64,256]{2,1,0:T(8,128)}, f32[16,64,256]{2,1,0:T(8,128)}, /*index=5*/s32[]{:T(128)}, s32[]{:T(128)}) while((s32[]{:T(128)}, f32[64,256]{1,0:T(8,128)S(1)}, s32[]{:T(128)}, f32[16,64,256]{2,1,0:T(8,128)}, f32[16,64,256]{2,1,0:T(8,128)}, ...), condition=%wide.region_4.5_spmd.clone, body=%wide.region_3.4_spmd.clone.sunk | while | flops 65540 | bytes 262245 | solution.py:40
  311.7 23.3 %while.90 = (s32[]{:T(128)}, f32[64,256]{1,0:T(8,128)S(1)}, f32[64,256]{1,0:T(8,128)}, f32[16,64,256]{2,1,0:T(8,128)S(1)}, f32[16,64,256]{2,1,0:T(8,128)S(1)}, /*index=5*/s32[]{:T(128)}, s32[]{:T(128)}, s32[]{:T(128)}) while((s32[]{:T(128)}, f32[64,256]{1,0:T(8,128)S(1)}, f32[64,256]{1,0:T(8,128)}, f32[16,64,256]{2,1,0:T(8,128)S(1)}, ...), condition=%wide.region_8.9_spmd.clone, body=%wide.region_7.8_spmd.clone.sunk | while | flops 81924 | bytes 393327 | solution.py:105
  336.4 67.3 %all-gather.16.cloned.1.call-done = f32[1024,256]{1,0:T(8,128)} async-done(((f32[64,256]{1,0:T(8,128)}), f32[1024,256]{1,0:T(8,128)}) %all-gather.16.cloned.1.call-update) | async-done | bytes 1048592 | tf_op jit(solution)/shard_map/all_gather | solution.py:28
  405.0 68.6 %all-gather.18.cloned.1.call-done = f32[1024,256]{1,0:T(8,128)} async-done(((f32[64,256]{1,0:T(8,128)}), f32[1024,256]{1,0:T(8,128)}) %all-gather.18.cloned.1.call-update) | async-done | bytes 1048592 | tf_op jit(solution)/shard_map/all_gather | solution.py:28
  475.9 13.6 %while.91 = (s32[]{:T(128)}, f32[64,256]{1,0:T(8,128)S(1)}, s32[]{:T(128)}, f32[16,64,256]{2,1,0:T(8,128)S(1)}, f32[16,64,256]{2,1,0:T(8,128)}, /*index=5*/s32[]{:T(128)}, s32[]{:T(128)}) while((s32[]{:T(128)}, f32[64,256]{1,0:T(8,128)S(1)}, s32[]{:T(128)}, f32[16,64,256]{2,1,0:T(8,128)S(1)}, f32[16,64,256]{2,1,0:T(8,128)}, ...), condition=%wide.region_10.11_spmd.clone, body=%wide.region_9.10_spmd.clone.sunk | while | flops 65540 | bytes 262245 | solution.py:40
  492.2 6.4 %broadcast_in_dim.31 = f32[16,2,2,2,256,2]{5,4,1,0,3,2:T(8,128)} broadcast(f32[16,2,256]{2,0,1:T(8,128)S(1)} %fusion.59), dimensions={0,2,4} | broadcast | bytes 294912 | tf_op jit(solution)/shard_map/broadcast_in_dim | solution.py:151
  498.7 12.7 %reshape.131 = f32[32,4,512]{2,0,1:T(8,128)S(1)} reshape(f32[16,2,2,2,256,2]{5,4,1,0,3,2:T(8,128)} %broadcast_in_dim.31) | data formatting | bytes 524288 | tf_op jit(solution)/shard_map/reshape | solution.py:154
  511.4 4.2 collective-permute-start.12
  517.6 4.8 collective-permute-done.13
  524.4 2.4 collective-permute-start.15
  526.8 5.4 collective-permute-done.15
  534.5 3.9 collective-permute-start.17
  538.4 2.8 collective-permute-done.17
  543.2 2.4 collective-permute-start.19
  545.6 5.4 collective-permute-done.19
  (178 shorter events, 94.0 us)
Async XLA Ops:
  6.5 145.5 %all-gather.10.cloned.1.call-start = ((), (), s32[]{:S(2)}) async-start(), calls=%async_computation | async-start | bytes 1081344 | tf_op jit(solution)/shard_map/all_gather | solution.py:126
  7.3 6.9 %collective-permute-start = (f32[1,4,512]{2,0,1:T(1,128)S(1)}, f32[1,4,512]{2,0,1:T(1,128)S(1)}, u32[]{:S(2)}, u32[]{:S(2)}) collective-permute-start(f32[1,4,512]{2,0,1:T(1,128)S(1)} %copy.19), channel_id=1, source_target_pairs={{32,0},{64,32},{96,64},{128,96},{160,128},{192,160},{224,192},{256... | collective-permute-start | bytes 24584 | tf_op jit(solution)/shard_map/ppermute | solution.py:21
  9.3 6.8 %collective-permute-start.1 = (f32[1,4,512]{2,0,1:T(1,128)S(1)}, f32[1,4,512]{2,0,1:T(1,128)S(1)}, u32[]{:S(2)}, u32[]{:S(2)}) collective-permute-start(f32[1,4,512]{2,0,1:T(1,128)S(1)} %copy.21), channel_id=1, source_target_pairs={{0,32},{32,64},{64,96},{96,128},{128,160},{160,192},{192,224},{224... | collective-permute-start | bytes 24584 | tf_op jit(solution)/shard_map/ppermute | solution.py:20
  16.1 5.4 collective-permute-start.2
  19.5 7.9 %collective-permute-start.3 = (f32[34,1,512]{2,0,1:T(8,128)S(1)}, f32[34,1,512]{2,0,1:T(8,128)S(1)}, u32[]{:S(2)}, u32[]{:S(2)}) collective-permute-start(f32[34,1,512]{2,0,1:T(8,128)S(1)} %get-tuple-element.612), channel_id=1, source_target_pairs={{0,1},{1,2},{2,3},{3,4},{4,5},{5,6},{6,7},{7,8},{8,9},{9,10},{10,1... | collective-permute-start | bytes 208904 | tf_op jit(solution)/shard_map/ppermute | solution.py:20
  28.6 5.9 %collective-permute-start.4 = (f32[1,4,512]{2,0,1:T(1,128)S(1)}, f32[1,4,512]{2,0,1:T(1,128)S(1)}, u32[]{:S(2)}, u32[]{:S(2)}) collective-permute-start(f32[1,4,512]{2,0,1:T(1,128)S(1)} %get-tuple-element.620), channel_id=1, source_target_pairs={{32,0},{64,32},{96,64},{128,96},{160,128},{192,160},{224,192},{256... | collective-permute-start | bytes 24584 | tf_op jit(solution)/shard_map/ppermute | solution.py:21
  30.8 6.8 %collective-permute-start.5 = (f32[1,4,512]{2,0,1:T(1,128)S(1)}, f32[1,4,512]{2,0,1:T(1,128)S(1)}, u32[]{:S(2)}, u32[]{:S(2)}) collective-permute-start(f32[1,4,512]{2,0,1:T(1,128)S(1)} %get-tuple-element.619), channel_id=1, source_target_pairs={{0,32},{32,64},{64,96},{96,128},{128,160},{160,192},{192,224},{224... | collective-permute-start | bytes 24584 | tf_op jit(solution)/shard_map/ppermute | solution.py:20
  37.6 4.3 collective-permute-start.6
  39.6 7.9 %collective-permute-start.7 = (f32[34,1,512]{2,0,1:T(8,128)S(1)}, f32[34,1,512]{2,0,1:T(8,128)S(1)}, u32[]{:S(2)}, u32[]{:S(2)}) collective-permute-start(f32[34,1,512]{2,0,1:T(8,128)S(1)} %get-tuple-element.610), channel_id=1, source_target_pairs={{0,1},{1,2},{2,3},{3,4},{4,5},{5,6},{6,7},{7,8},{8,9},{9,10},{10,1... | collective-permute-start | bytes 208904 | tf_op jit(solution)/shard_map/ppermute | solution.py:20
  48.7 5.9 %collective-permute-start.8 = (f32[1,4,512]{2,0,1:T(1,128)S(1)}, f32[1,4,512]{2,0,1:T(1,128)S(1)}, u32[]{:S(2)}, u32[]{:S(2)}) collective-permute-start(f32[1,4,512]{2,0,1:T(1,128)S(1)} %get-tuple-element.618), channel_id=1, source_target_pairs={{32,0},{64,32},{96,64},{128,96},{160,128},{192,160},{224,192},{256... | collective-permute-start | bytes 24584 | tf_op jit(solution)/shard_map/ppermute | solution.py:21
  50.6 6.8 %collective-permute-start.9 = (f32[1,4,512]{2,0,1:T(1,128)S(1)}, f32[1,4,512]{2,0,1:T(1,128)S(1)}, u32[]{:S(2)}, u32[]{:S(2)}) collective-permute-start(f32[1,4,512]{2,0,1:T(1,128)S(1)} %get-tuple-element.617), channel_id=1, source_target_pairs={{0,32},{32,64},{64,96},{96,128},{128,160},{160,192},{192,224},{224... | collective-permute-start | bytes 24584 | tf_op jit(solution)/shard_map/ppermute | solution.py:20
  57.4 4.3 collective-permute-start.10
  59.3 7.9 %collective-permute-start.11 = (f32[34,1,512]{2,0,1:T(8,128)S(1)}, f32[34,1,512]{2,0,1:T(8,128)S(1)}, u32[]{:S(2)}, u32[]{:S(2)}) collective-permute-start(f32[34,1,512]{2,0,1:T(8,128)S(1)} %get-tuple-element.608), channel_id=1, source_target_pairs={{0,1},{1,2},{2,3},{3,4},{4,5},{5,6},{6,7},{7,8},{8,9},{9,10},{10,1... | collective-permute-start | bytes 208904 | tf_op jit(solution)/shard_map/ppermute | solution.py:20
  94.1 132.7 %all-gather.14.cloned.1.call-start = ((), (), s32[]{:S(2)}) async-start(), calls=%async_computation.2 | async-start | bytes 1114112 | tf_op jit(solution)/shard_map/all_gather | solution.py:28
  158.0 0.6 copy-start.3
  158.0 0.7 copy-start.2
  158.7 138.1 %all-gather.12.cloned.1.call-start = ((), (), s32[]{:S(2)}) async-start(), calls=%async_computation.1 | async-start | bytes 1114112 | tf_op jit(solution)/shard_map/all_gather | solution.py:28
  159.4 244.2 %all-gather.16.cloned.1.call-start = ((), (), s32[]{:S(2)}) async-start(), calls=%async_computation.3 | async-start | bytes 1114112 | tf_op jit(solution)/shard_map/all_gather | solution.py:28
  334.9 0.6 copy-start.1
  335.6 137.9 %all-gather.18.cloned.1.call-start = ((), (), s32[]{:S(2)}) async-start(), calls=%async_computation.4 | async-start | bytes 1114112 | tf_op jit(solution)/shard_map/all_gather | solution.py:28
  492.2 40.0 %copy-start = (f32[32,4,512]{2,1,0:T(4,128)S(1)}, f32[32,4,512]{2,1,0:T(4,128)}, u32[]{:S(2)}) copy-start(f32[32,4,512]{2,1,0:T(4,128)} %param.14) | copy-start | bytes 786436
  511.4 6.1 %collective-permute-start.12 = (f32[1,4,512]{2,0,1:T(1,128)S(1)}, f32[1,4,512]{2,0,1:T(1,128)S(1)}, u32[]{:S(2)}, u32[]{:S(2)}) collective-permute-start(f32[1,4,512]{2,0,1:T(1,128)S(1)} %get-tuple-element.616), channel_id=1, source_target_pairs={{32,0},{64,32},{96,64},{128,96},{160,128},{192,160},{224,192},{256... | collective-permute-start | bytes 24584 | tf_op jit(solution)/shard_map/ppermute | solution.py:21
  515.6 6.8 %collective-permute-start.13 = (f32[1,4,512]{2,0,1:T(1,128)S(1)}, f32[1,4,512]{2,0,1:T(1,128)S(1)}, u32[]{:S(2)}, u32[]{:S(2)}) collective-permute-start(f32[1,4,512]{2,0,1:T(1,128)S(1)} %get-tuple-element.615), channel_id=1, source_target_pairs={{0,32},{32,64},{64,96},{96,128},{128,160},{160,192},{192,224},{224... | collective-permute-start | bytes 24584 | tf_op jit(solution)/shard_map/ppermute | solution.py:20
  522.4 4.3 collective-permute-start.14
  524.4 7.9 %collective-permute-start.15 = (f32[34,1,512]{2,0,1:T(8,128)S(1)}, f32[34,1,512]{2,0,1:T(8,128)S(1)}, u32[]{:S(2)}, u32[]{:S(2)}) collective-permute-start(f32[34,1,512]{2,0,1:T(8,128)S(1)} %get-tuple-element.606), channel_id=1, source_target_pairs={{0,1},{1,2},{2,3},{3,4},{4,5},{5,6},{6,7},{7,8},{8,9},{9,10},{10,1... | collective-permute-start | bytes 208904 | tf_op jit(solution)/shard_map/ppermute | solution.py:20
  532.5 5.9 %collective-permute-start.16 = (f32[1,4,512]{2,0,1:T(1,128)S(1)}, f32[1,4,512]{2,0,1:T(1,128)S(1)}, u32[]{:S(2)}, u32[]{:S(2)}) collective-permute-start(f32[1,4,512]{2,0,1:T(1,128)S(1)} %get-tuple-element.614), channel_id=1, source_target_pairs={{32,0},{64,32},{96,64},{128,96},{160,128},{192,160},{224,192},{256... | collective-permute-start | bytes 24584 | tf_op jit(solution)/shard_map/ppermute | solution.py:21
  534.5 6.8 %collective-permute-start.17 = (f32[1,4,512]{2,0,1:T(1,128)S(1)}, f32[1,4,512]{2,0,1:T(1,128)S(1)}, u32[]{:S(2)}, u32[]{:S(2)}) collective-permute-start(f32[1,4,512]{2,0,1:T(1,128)S(1)} %get-tuple-element.613), channel_id=1, source_target_pairs={{0,32},{32,64},{64,96},{96,128},{128,160},{160,192},{192,224},{224... | collective-permute-start | bytes 24584 | tf_op jit(solution)/shard_map/ppermute | solution.py:20
  541.3 4.3 collective-permute-start.18
  543.2 7.9 %collective-permute-start.19 = (f32[34,1,512]{2,0,1:T(8,128)S(1)}, f32[34,1,512]{2,0,1:T(8,128)S(1)}, u32[]{:S(2)}, u32[]{:S(2)}) collective-permute-start(f32[34,1,512]{2,0,1:T(8,128)S(1)} %get-tuple-element.604), channel_id=1, source_target_pairs={{0,1},{1,2},{2,3},{3,4},{4,5},{5,6},{6,7},{7,8},{8,9},{9,10},{10,1... | collective-permute-start | bytes 208904 | tf_op jit(solution)/shard_map/ppermute | solution.py:20
Sparse Core Ops, SparseCore 0:
  94.2 57.8 all-gather.9
  158.8 67.9 all-gather.13
  228.9 67.9 all-gather.11
  335.7 67.9 all-gather.15
  405.6 67.9 all-gather.17
where the time goes:
time: 562 us; the launch traced here: 559 us
  waiting for transfers between devices  374 us (67%)
  other arithmetic  64.6 us (11%)
  starting transfers between devices  52.4 us (9%)
  local copies, waits for them, and re-layouts  45 us (8%)
  between operations  13.7 us (2%)
  matrix products  7.03 us (1%)
    all_gather x4, waiting for transfers between devices, carried_in(): pieces = jax.tree.map(lambda part: lax.all_gather(part, axis), value)  273 us
    all_gather x1, waiting for transfers between devices, coarse_solve(): whole = lax.all_gather(coarse, 'xy', axis=1, tiled=True)  56.8 us
    ppermute x10, waiting for transfers between devices, with_halo(): before = lax.ppermute(last, axis, up)  43.1 us
    ppermute x10, starting transfers between devices, with_halo(): before = lax.ppermute(last, axis, up)  28.7 us
    select_n x30, other arithmetic, step(): jnp.where(position < mine, new, old)  27 us
    ppermute x10, starting transfers between devices, with_halo(): after = lax.ppermute(initial, axis, down)  23.4 us
    add x16, other arithmetic, down_step(): return ((pivot * carry[0], value + pivot * carry[1]), None)  23.2 us
    reshape x1, local copies, waits for them, and re-layouts, body(): residual.reshape(height // 2, 2, width // 2, 2, depth_y // 2, 2)  18.1 us
  transfers between devices with their start and end apart: 25, of which 16 were waited for; matrix products, arithmetic and copies ran while one was open for 1% of the time, Pallas kernels for 0%

commit v1 on v0

--- a/solution.py
+++ b/solution.py
@@ -123,7 +123,9 @@
     table_x = sine_table(total_rows)
     table_y = sine_table(cols)
     modes_x = eigenvalues(total_rows, total_rows)
-    whole = lax.all_gather(coarse, "xy", axis=1, tiled=True)
+    whole = jnp.concatenate(
+        lax.all_to_all(jnp.stack([coarse] * lax.axis_size("xy")), "xy", 0, 0), axis=1
+    )
     spec = jnp.dot(whole.reshape(-1, cols), table_y, precision=HIGH).reshape(
         planes, total_rows, cols
     )

time: 562 us -> 524 us (0.932)
  waiting for transfers between devices: 374 us -> 333 us
    all_gather x1 -> x0, waiting for transfers between devices: 56.8 us -> none  [coarse_solve(): whole = lax.all_gather(coarse, 'xy', axis=1, tiled=True)]
    all_to_all x0 -> x1, waiting for transfers between devices: none -> 14.2 us  [coarse_solve(): lax.all_to_all(jnp.stack([coarse] * lax.axis_size('xy')), 'xy', 0, 0)]
where the time goes in v1:
time: 524 us; the launch traced here: 521 us
  waiting for transfers between devices  333 us (64%)
  other arithmetic  64 us (12%)
  starting transfers between devices  57.1 us (11%)
  local copies, waits for them, and re-layouts  46.1 us (9%)
  between operations  13.7 us (3%)
  matrix products  5.81 us (1%)
    all_gather x4, waiting for transfers between devices, carried_in(): pieces = jax.tree.map(lambda part: lax.all_gather(part, axis), value)  274 us
    ppermute x10, waiting for transfers between devices, with_halo(): before = lax.ppermute(last, axis, up)  43 us
    ppermute x10, starting transfers between devices, with_halo(): before = lax.ppermute(last, axis, up)  28.7 us
    select_n x30, other arithmetic, step(): jnp.where(position < mine, new, old)  27 us
    ppermute x10, starting transfers between devices, with_halo(): after = lax.ppermute(initial, axis, down)  23.4 us
    add x16, other arithmetic, down_step(): return ((pivot * carry[0], value + pivot * carry[1]), None)  23.2 us
    reshape x1, local copies, waits for them, and re-layouts, body(): residual.reshape(height // 2, 2, width // 2, 2, depth_y // 2, 2)  18.1 us
    all_to_all x1, waiting for transfers between devices, coarse_solve(): lax.all_to_all(jnp.stack([coarse] * lax.axis_size('xy')), 'xy', 0, 0)  14.2 us
  transfers between devices with their start and end apart: 25, of which 16 were waited for; matrix products, arithmetic and copies ran while one was open for 1% of the time, Pallas kernels for 0%

profile of v1, /device:TPU:134, one launch (start us, length us, event | category | flops | bytes accessed | tf_op | source)
XLA Modules:
  0.0 521.2 jit_solution(14380890118402068433)
XLA Ops:
  9.3 3.8 collective-permute-start.1
  16.1 3.4 collective-permute-start.2
  21.5 5.8 %collective-permute-done.3 = f32[34,1,512]{2,0,1:T(8,128)S(1)} collective-permute-done((f32[34,1,512]{2,0,1:T(8,128)S(1)}, f32[34,1,512]{2,0,1:T(8,128)S(1)}, u32[]{:S(2)}, u32[]{:S(2)}) %collective-permute-start.3) | collective-permute-done | bytes 69664 | tf_op jit(solution)/shard_map/ppermute | solution.py:20
  30.8 3.6 collective-permute-start.5
  34.5 3.1 collective-permute-done.5
  39.6 2.4 collective-permute-start.7
  42.0 5.4 %collective-permute-done.7 = f32[34,1,512]{2,0,1:T(8,128)S(1)} collective-permute-done((f32[34,1,512]{2,0,1:T(8,128)S(1)}, f32[34,1,512]{2,0,1:T(8,128)S(1)}, u32[]{:S(2)}, u32[]{:S(2)}) %collective-permute-start.7) | collective-permute-done | bytes 69664 | tf_op jit(solution)/shard_map/ppermute | solution.py:20
  50.6 3.9 collective-permute-start.9
  54.5 2.8 collective-permute-done.9
  59.3 2.4 collective-permute-start.11
  61.8 5.4 %collective-permute-done.11 = f32[34,1,512]{2,0,1:T(8,128)S(1)} collective-permute-done((f32[34,1,512]{2,0,1:T(8,128)S(1)}, f32[34,1,512]{2,0,1:T(8,128)S(1)}, u32[]{:S(2)}, u32[]{:S(2)}) %collective-permute-start.11) | collective-permute-done | bytes 69664 | tf_op jit(solution)/shard_map/ppermute | solution.py:20
  68.4 18.1 %reshape.134 = f32[16,2,2,2,256,2]{5,4,1,0,3,2:T(8,128)} reshape(f32[32,4,512]{2,0,1:T(8,128)S(1)} %fusion.23) | data formatting | bytes 524288 | tf_op jit(solution)/shard_map/reshape | solution.py:151
  86.5 7.0 %reduce_sum.9 = f32[16,2,256]{2,0,1:T(8,128)S(1)} reduce(f32[16,2,2,2,256,2]{5,4,1,0,3,2:T(8,128)} %reshape.134, f32[]{:T(128)} %constant.201.clone.1), dimensions={1,3,5}, to_apply=%region_0.1 | reduce | flops 57344 | bytes 294916 | tf_op jit(solution)/shard_map/reduce_sum | solution.py:151
  94.6 4.7 all-to-all-start
  100.4 14.2 %all-to-all-done = f32[32,16,2,256]{3,1,2,0:T(8,128)S(1)} async-done(((f32[32,16,2,256]{3,1,2,0:T(8,128)}), f32[32,16,2,256]{3,1,2,0:T(8,128)S(1)}, u32[]{:S(2)}, u32[]{:S(2)}) %all-to-all-start) | async-done | bytes 1048608 | tf_op jit(solution)/shard_map/all_to_all | solution.py:127
  114.6 2.5 fusion.6
  120.8 68.5 %all-gather.9.cloned.1.call-done = f32[1024,256]{1,0:T(8,128)} async-done(((f32[64,256]{1,0:T(8,128)}), f32[1024,256]{1,0:T(8,128)}) %all-gather.9.cloned.1.call-update) | async-done | bytes 1048592 | tf_op jit(solution)/shard_map/all_gather | solution.py:28
  189.3 70.0 %all-gather.11.cloned.1.call-done = f32[1024,256]{1,0:T(8,128)} async-done(((f32[64,256]{1,0:T(8,128)}), f32[1024,256]{1,0:T(8,128)}) %all-gather.11.cloned.1.call-update) | async-done | bytes 1048592 | tf_op jit(solution)/shard_map/all_gather | solution.py:28
  259.3 14.0 %while.89 = (s32[]{:T(128)}, f32[64,256]{1,0:T(8,128)S(1)}, s32[]{:T(128)}, f32[16,64,256]{2,1,0:T(8,128)}, f32[16,64,256]{2,1,0:T(8,128)}, /*index=5*/s32[]{:T(128)}, s32[]{:T(128)}) while((s32[]{:T(128)}, f32[64,256]{1,0:T(8,128)S(1)}, s32[]{:T(128)}, f32[16,64,256]{2,1,0:T(8,128)}, f32[16,64,256]{2,1,0:T(8,128)}, ...), condition=%wide.region_4.5_spmd.clone, body=%wide.region_3.4_spmd.clone.sunk | while | flops 65540 | bytes 262245 | solution.py:40
  274.1 23.3 %while.90 = (s32[]{:T(128)}, f32[64,256]{1,0:T(8,128)S(1)}, f32[64,256]{1,0:T(8,128)}, f32[16,64,256]{2,1,0:T(8,128)S(1)}, f32[16,64,256]{2,1,0:T(8,128)S(1)}, /*index=5*/s32[]{:T(128)}, s32[]{:T(128)}, s32[]{:T(128)}) while((s32[]{:T(128)}, f32[64,256]{1,0:T(8,128)S(1)}, f32[64,256]{1,0:T(8,128)}, f32[16,64,256]{2,1,0:T(8,128)S(1)}, ...), condition=%wide.region_8.9_spmd.clone, body=%wide.region_7.8_spmd.clone.sunk | while | flops 81924 | bytes 393327 | solution.py:105
  298.8 67.3 %all-gather.13.cloned.1.call-done = f32[1024,256]{1,0:T(8,128)} async-done(((f32[64,256]{1,0:T(8,128)}), f32[1024,256]{1,0:T(8,128)}) %all-gather.13.cloned.1.call-update) | async-done | bytes 1048592 | tf_op jit(solution)/shard_map/all_gather | solution.py:28
  367.4 68.6 %all-gather.15.cloned.1.call-done = f32[1024,256]{1,0:T(8,128)} async-done(((f32[64,256]{1,0:T(8,128)}), f32[1024,256]{1,0:T(8,128)}) %all-gather.15.cloned.1.call-update) | async-done | bytes 1048592 | tf_op jit(solution)/shard_map/all_gather | solution.py:28
  438.3 13.6 %while.91 = (s32[]{:T(128)}, f32[64,256]{1,0:T(8,128)S(1)}, s32[]{:T(128)}, f32[16,64,256]{2,1,0:T(8,128)S(1)}, f32[16,64,256]{2,1,0:T(8,128)}, /*index=5*/s32[]{:T(128)}, s32[]{:T(128)}) while((s32[]{:T(128)}, f32[64,256]{1,0:T(8,128)S(1)}, s32[]{:T(128)}, f32[16,64,256]{2,1,0:T(8,128)S(1)}, f32[16,64,256]{2,1,0:T(8,128)}, ...), condition=%wide.region_10.11_spmd.clone, body=%wide.region_9.10_spmd.clone.sunk | while | flops 65540 | bytes 262245 | solution.py:40
  454.7 6.4 %broadcast_in_dim.31 = f32[16,2,2,2,256,2]{5,4,1,0,3,2:T(8,128)} broadcast(f32[16,2,256]{2,0,1:T(8,128)S(1)} %fusion.59), dimensions={0,2,4} | broadcast | bytes 294912 | tf_op jit(solution)/shard_map/broadcast_in_dim | solution.py:153
  461.1 12.7 %reshape.136 = f32[32,4,512]{2,0,1:T(8,128)S(1)} reshape(f32[16,2,2,2,256,2]{5,4,1,0,3,2:T(8,128)} %broadcast_in_dim.31) | data formatting | bytes 524288 | tf_op jit(solution)/shard_map/reshape | solution.py:156
  473.9 4.2 collective-permute-start.12
  480.1 4.8 collective-permute-done.13
  486.8 2.4 collective-permute-start.15
  489.2 5.4 %collective-permute-done.15 = f32[34,1,512]{2,0,1:T(8,128)S(1)} collective-permute-done((f32[34,1,512]{2,0,1:T(8,128)S(1)}, f32[34,1,512]{2,0,1:T(8,128)S(1)}, u32[]{:S(2)}, u32[]{:S(2)}) %collective-permute-start.15) | collective-permute-done | bytes 69664 | tf_op jit(solution)/shard_map/ppermute | solution.py:20
  496.9 3.9 collective-permute-start.17
  500.9 2.8 collective-permute-done.17
  508.1 5.4 %collective-permute-done.19 = f32[34,1,512]{2,0,1:T(8,128)S(1)} collective-permute-done((f32[34,1,512]{2,0,1:T(8,128)S(1)}, f32[34,1,512]{2,0,1:T(8,128)S(1)}, u32[]{:S(2)}, u32[]{:S(2)}) %collective-permute-start.19) | collective-permute-done | bytes 69664 | tf_op jit(solution)/shard_map/ppermute | solution.py:20
  (178 shorter events, 96.9 us)
Async XLA Ops:
  7.3 6.9 %collective-permute-start = (f32[1,4,512]{2,0,1:T(1,128)S(1)}, f32[1,4,512]{2,0,1:T(1,128)S(1)}, u32[]{:S(2)}, u32[]{:S(2)}) collective-permute-start(f32[1,4,512]{2,0,1:T(1,128)S(1)} %copy.5), channel_id=1, source_target_pairs={{32,0},{64,32},{96,64},{128,96},{160,128},{192,160},{224,192},{256... | collective-permute-start | bytes 24584 | tf_op jit(solution)/shard_map/ppermute | solution.py:21
  9.3 6.8 %collective-permute-start.1 = (f32[1,4,512]{2,0,1:T(1,128)S(1)}, f32[1,4,512]{2,0,1:T(1,128)S(1)}, u32[]{:S(2)}, u32[]{:S(2)}) collective-permute-start(f32[1,4,512]{2,0,1:T(1,128)S(1)} %copy.7), channel_id=1, source_target_pairs={{0,32},{32,64},{64,96},{96,128},{128,160},{160,192},{192,224},{224... | collective-permute-start | bytes 24584 | tf_op jit(solution)/shard_map/ppermute | solution.py:20
  16.1 5.4 %collective-permute-start.2 = (f32[34,1,512]{2,0,1:T(8,128)S(1)}, f32[34,1,512]{2,0,1:T(8,128)S(1)}, u32[]{:S(2)}, u32[]{:S(2)}) collective-permute-start(f32[34,1,512]{2,0,1:T(8,128)S(1)} %get-tuple-element.611), channel_id=1, source_target_pairs={{1,0},{2,1},{3,2},{4,3},{5,4},{6,5},{7,6},{8,7},{9,8},{10,9},{11,1... | collective-permute-start | bytes 208904 | tf_op jit(solution)/shard_map/ppermute | solution.py:21
  19.5 7.9 %collective-permute-start.3 = (f32[34,1,512]{2,0,1:T(8,128)S(1)}, f32[34,1,512]{2,0,1:T(8,128)S(1)}, u32[]{:S(2)}, u32[]{:S(2)}) collective-permute-start(f32[34,1,512]{2,0,1:T(8,128)S(1)} %get-tuple-element.612), channel_id=1, source_target_pairs={{0,1},{1,2},{2,3},{3,4},{4,5},{5,6},{6,7},{7,8},{8,9},{9,10},{10,1... | collective-permute-start | bytes 208904 | tf_op jit(solution)/shard_map/ppermute | solution.py:20
  28.6 5.9 %collective-permute-start.4 = (f32[1,4,512]{2,0,1:T(1,128)S(1)}, f32[1,4,512]{2,0,1:T(1,128)S(1)}, u32[]{:S(2)}, u32[]{:S(2)}) collective-permute-start(f32[1,4,512]{2,0,1:T(1,128)S(1)} %get-tuple-element.620), channel_id=1, source_target_pairs={{32,0},{64,32},{96,64},{128,96},{160,128},{192,160},{224,192},{256... | collective-permute-start | bytes 24584 | tf_op jit(solution)/shard_map/ppermute | solution.py:21
  30.8 6.8 %collective-permute-start.5 = (f32[1,4,512]{2,0,1:T(1,128)S(1)}, f32[1,4,512]{2,0,1:T(1,128)S(1)}, u32[]{:S(2)}, u32[]{:S(2)}) collective-permute-start(f32[1,4,512]{2,0,1:T(1,128)S(1)} %get-tuple-element.619), channel_id=1, source_target_pairs={{0,32},{32,64},{64,96},{96,128},{128,160},{160,192},{192,224},{224... | collective-permute-start | bytes 24584 | tf_op jit(solution)/shard_map/ppermute | solution.py:20
  37.6 4.3 collective-permute-start.6
  39.6 7.9 %collective-permute-start.7 = (f32[34,1,512]{2,0,1:T(8,128)S(1)}, f32[34,1,512]{2,0,1:T(8,128)S(1)}, u32[]{:S(2)}, u32[]{:S(2)}) collective-permute-start(f32[34,1,512]{2,0,1:T(8,128)S(1)} %get-tuple-element.610), channel_id=1, source_target_pairs={{0,1},{1,2},{2,3},{3,4},{4,5},{5,6},{6,7},{7,8},{8,9},{9,10},{10,1... | collective-permute-start | bytes 208904 | tf_op jit(solution)/shard_map/ppermute | solution.py:20
  48.7 5.9 %collective-permute-start.8 = (f32[1,4,512]{2,0,1:T(1,128)S(1)}, f32[1,4,512]{2,0,1:T(1,128)S(1)}, u32[]{:S(2)}, u32[]{:S(2)}) collective-permute-start(f32[1,4,512]{2,0,1:T(1,128)S(1)} %get-tuple-element.618), channel_id=1, source_target_pairs={{32,0},{64,32},{96,64},{128,96},{160,128},{192,160},{224,192},{256... | collective-permute-start | bytes 24584 | tf_op jit(solution)/shard_map/ppermute | solution.py:21
  50.6 6.8 %collective-permute-start.9 = (f32[1,4,512]{2,0,1:T(1,128)S(1)}, f32[1,4,512]{2,0,1:T(1,128)S(1)}, u32[]{:S(2)}, u32[]{:S(2)}) collective-permute-start(f32[1,4,512]{2,0,1:T(1,128)S(1)} %get-tuple-element.617), channel_id=1, source_target_pairs={{0,32},{32,64},{64,96},{96,128},{128,160},{160,192},{192,224},{224... | collective-permute-start | bytes 24584 | tf_op jit(solution)/shard_map/ppermute | solution.py:20
  57.4 4.4 collective-permute-start.10
  59.3 7.9 %collective-permute-start.11 = (f32[34,1,512]{2,0,1:T(8,128)S(1)}, f32[34,1,512]{2,0,1:T(8,128)S(1)}, u32[]{:S(2)}, u32[]{:S(2)}) collective-permute-start(f32[34,1,512]{2,0,1:T(8,128)S(1)} %get-tuple-element.608), channel_id=1, source_target_pairs={{0,1},{1,2},{2,3},{3,4},{4,5},{5,6},{6,7},{7,8},{8,9},{9,10},{10,1... | collective-permute-start | bytes 208904 | tf_op jit(solution)/shard_map/ppermute | solution.py:20
  94.6 20.0 %all-to-all-start = ((f32[32,16,2,256]{3,1,2,0:T(8,128)}), f32[32,16,2,256]{3,1,2,0:T(8,128)S(1)}, u32[]{:S(2)}, u32[]{:S(2)}) async-start(f32[32,16,2,256]{3,1,2,0:T(8,128)} %stack.2), calls=%async_computation | async-start | bytes 2097152 | tf_op jit(solution)/shard_map/all_to_all | solution.py:127
  99.3 90.0 %all-gather.9.cloned.1.call-start = ((), (), s32[]{:S(2)}) async-start(), calls=%async_computation.1 | async-start | bytes 1114112 | tf_op jit(solution)/shard_map/all_gather | solution.py:28
  119.3 0.6 copy-start.2
  119.3 0.7 copy-start.3
  120.0 139.3 %all-gather.11.cloned.1.call-start = ((), (), s32[]{:S(2)}) async-start(), calls=%async_computation.2 | async-start | bytes 1114112 | tf_op jit(solution)/shard_map/all_gather | solution.py:28
  120.7 245.4 %all-gather.13.cloned.1.call-start = ((), (), s32[]{:S(2)}) async-start(), calls=%async_computation.3 | async-start | bytes 1114112 | tf_op jit(solution)/shard_map/all_gather | solution.py:28
  297.4 0.6 copy-start.1
  298.0 138.0 %all-gather.15.cloned.1.call-start = ((), (), s32[]{:S(2)}) async-start(), calls=%async_computation.4 | async-start | bytes 1114112 | tf_op jit(solution)/shard_map/all_gather | solution.py:28
  454.7 40.0 %copy-start = (f32[32,4,512]{2,1,0:T(4,128)S(1)}, f32[32,4,512]{2,1,0:T(4,128)}, u32[]{:S(2)}) copy-start(f32[32,4,512]{2,1,0:T(4,128)} %param.14) | copy-start | bytes 786436
  473.9 6.1 %collective-permute-start.12 = (f32[1,4,512]{2,0,1:T(1,128)S(1)}, f32[1,4,512]{2,0,1:T(1,128)S(1)}, u32[]{:S(2)}, u32[]{:S(2)}) collective-permute-start(f32[1,4,512]{2,0,1:T(1,128)S(1)} %get-tuple-element.616), channel_id=1, source_target_pairs={{32,0},{64,32},{96,64},{128,96},{160,128},{192,160},{224,192},{256... | collective-permute-start | bytes 24584 | tf_op jit(solution)/shard_map/ppermute | solution.py:21
  478.1 6.8 %collective-permute-start.13 = (f32[1,4,512]{2,0,1:T(1,128)S(1)}, f32[1,4,512]{2,0,1:T(1,128)S(1)}, u32[]{:S(2)}, u32[]{:S(2)}) collective-permute-start(f32[1,4,512]{2,0,1:T(1,128)S(1)} %get-tuple-element.615), channel_id=1, source_target_pairs={{0,32},{32,64},{64,96},{96,128},{128,160},{160,192},{192,224},{224... | collective-permute-start | bytes 24584 | tf_op jit(solution)/shard_map/ppermute | solution.py:20
  484.9 4.3 collective-permute-start.14
  486.8 7.9 %collective-permute-start.15 = (f32[34,1,512]{2,0,1:T(8,128)S(1)}, f32[34,1,512]{2,0,1:T(8,128)S(1)}, u32[]{:S(2)}, u32[]{:S(2)}) collective-permute-start(f32[34,1,512]{2,0,1:T(8,128)S(1)} %get-tuple-element.606), channel_id=1, source_target_pairs={{0,1},{1,2},{2,3},{3,4},{4,5},{5,6},{6,7},{7,8},{8,9},{9,10},{10,1... | collective-permute-start | bytes 208904 | tf_op jit(solution)/shard_map/ppermute | solution.py:20
  495.0 5.9 %collective-permute-start.16 = (f32[1,4,512]{2,0,1:T(1,128)S(1)}, f32[1,4,512]{2,0,1:T(1,128)S(1)}, u32[]{:S(2)}, u32[]{:S(2)}) collective-permute-start(f32[1,4,512]{2,0,1:T(1,128)S(1)} %get-tuple-element.614), channel_id=1, source_target_pairs={{32,0},{64,32},{96,64},{128,96},{160,128},{192,160},{224,192},{256... | collective-permute-start | bytes 24584 | tf_op jit(solution)/shard_map/ppermute | solution.py:21
  496.9 6.8 %collective-permute-start.17 = (f32[1,4,512]{2,0,1:T(1,128)S(1)}, f32[1,4,512]{2,0,1:T(1,128)S(1)}, u32[]{:S(2)}, u32[]{:S(2)}) collective-permute-start(f32[1,4,512]{2,0,1:T(1,128)S(1)} %get-tuple-element.613), channel_id=1, source_target_pairs={{0,32},{32,64},{64,96},{96,128},{128,160},{160,192},{192,224},{224... | collective-permute-start | bytes 24584 | tf_op jit(solution)/shard_map/ppermute | solution.py:20
  503.7 4.3 collective-permute-start.18
  505.6 7.9 %collective-permute-start.19 = (f32[34,1,512]{2,0,1:T(8,128)S(1)}, f32[34,1,512]{2,0,1:T(8,128)S(1)}, u32[]{:S(2)}, u32[]{:S(2)}) collective-permute-start(f32[34,1,512]{2,0,1:T(8,128)S(1)} %get-tuple-element.604), channel_id=1, source_target_pairs={{0,1},{1,2},{2,3},{3,4},{4,5},{5,6},{6,7},{7,8},{8,9},{9,10},{10,1... | collective-permute-start | bytes 208904 | tf_op jit(solution)/shard_map/ppermute | solution.py:20
Sparse Core Ops, SparseCore 0:
  120.1 69.1 all-gather.8
  191.3 67.9 all-gather.10
  298.2 67.9 all-gather.12
  368.0 67.9 all-gather.14
